TPU v7x, 32 devices: a whole 2x2x4 slice. The times are simulated.
32 devices in a mesh: expert: 8 (over z, core), hid: 4 (over y, x).
Axes of the slice: x: 2, y: 2, z: 4, core: 2. Of those that a mesh axis runs over, the one named last changes fastest.
Arguments:
- tokens: bfloat16 [64, 3584], P('expert', 'hid'), may hold values from -6 to 6
- cotangent: bfloat16 [64, 3584], P('expert', 'hid'), may hold values from -6 to 6
- gate_prob: float32 [64, 8], P('expert'), may hold values from 0.1 to 1
- routes: int32 [64, 8], P('expert'), may hold values from 0 to 7, as said below
- slots: int32 [64, 8], P('expert'), may hold values from 0 to 8, as said below
- drop_seed: int32 [1], replicated, may hold values from 0 to 16777215
- layer_id: int32 [1], replicated, may hold values from 0 to 63
- w_gate: bfloat16 [8, 2560, 3584], P('expert', 'hid'), may hold values from -0.09375 to 0.09375
- w_up: bfloat16 [8, 2560, 3584], P('expert', 'hid'), may hold values from -0.09375 to 0.09375
- w_down: bfloat16 [8, 2560, 3584], P('expert', 'hid'), may hold values from -0.125 to 0.125
Outputs:
- grad_tokens: bfloat16 [64, 3584], P('expert', 'hid')
- grad_gate: bfloat16 [8, 2560, 3584], P('expert', 'hid')
- grad_up: bfloat16 [8, 2560, 3584], P('expert', 'hid')
- grad_down: bfloat16 [8, 2560, 3584], P('expert', 'hid')
Inputs may be any that keep to these rules, and one draw needn't show every extreme that they name: `routes`: each row names 8 different experts; one expert, drawn from the seed, is named by every token. Within one token group, the choices of each expert, taken in a priority order drawn from the seed, get slots 0, 1, 2 and so on, each slot at most once; those past 8 - 1 get the drop marker 8.
All inputs are finite; a program needn't handle non-finite values.
Results may differ from a plain program's by a relative error of at most 0.012.
Values may be sent and summed in bfloat16 or wider, within the bound.
No kernel may reach another device: no remote copies, remote signals or barrier semaphores. Data moves between devices by JAX's collectives and lax.ppermute only.
A program may use at most 64 MiB of HBM per device.

v0:
```python
import jax
import jax.numpy as jnp
from jax import lax
from jax.sharding import PartitionSpec as P

FF = 2560
CAP_SRC = 8
KEEP_FACTOR = 1024.0 / 922.0


def logical_shift(values, amount):
    return jnp.right_shift(values, amount) & (1 << 32 - amount) - 1


def keep_mask(counter, seed_value, layer_value):
    mixed = counter * -1640531535 + seed_value * 40503 + layer_value * 97
    mixed = mixed ^ logical_shift(mixed, 15)
    mixed = mixed * -2048144789
    mixed = mixed ^ logical_shift(mixed, 13)
    mixed = mixed * -1028477387
    mixed = mixed ^ logical_shift(mixed, 16)
    levels = logical_shift(mixed, 8) & 1023
    return jnp.where(levels >= 102, KEEP_FACTOR, 0.0).astype(jnp.float32)


def contract_rows(left, right):
    return lax.dot_general(
        left, right, (((0,), (0,)), ((), ())), preferred_element_type=jnp.float32
    )


def contract_cols(left, right):
    return lax.dot_general(
        left, right, (((1,), (1,)), ((), ())), preferred_element_type=jnp.float32
    )


def on_device(
    tokens, cotangent, gate_prob, routes, slots, drop_seed, layer_id, w_gate, w_up, w_down
):
    experts = lax.axis_size("expert")
    part_width = tokens.shape[1]
    capacity = experts * CAP_SRC
    local_units = w_gate.shape[1]
    target = jnp.where(slots < CAP_SRC, routes * CAP_SRC + slots, -1)
    slot_ids = jnp.arange(experts * CAP_SRC, dtype=jnp.int32)
    matches = target[None, :, :] == slot_ids[:, None, None]
    placed = jnp.any(matches, axis=2).astype(jnp.bfloat16)
    slot_gate = jnp.sum(jnp.where(matches, gate_prob[None, :, :], 0.0), axis=(1, 2))
    sent_x = jnp.dot(placed, tokens, preferred_element_type=jnp.float32).astype(jnp.bfloat16)
    plain_dy = jnp.dot(placed, cotangent, preferred_element_type=jnp.float32)
    sent_dy = (slot_gate[:, None] * plain_dy).astype(jnp.bfloat16)
    send_shape = (experts, CAP_SRC * part_width)
    recv_x, recv_dy = (
        lax.all_to_all(
            sent_x.reshape(send_shape), "expert", split_axis=0, concat_axis=0, tiled=True
        ),
        lax.all_to_all(
            sent_dy.reshape(send_shape), "expert", split_axis=0, concat_axis=0, tiled=True
        ),
    )
    rows_x, rows_dy = (
        lax.all_gather(recv_x.reshape(capacity, part_width), "hid", axis=1, tiled=True),
        lax.all_gather(recv_dy.reshape(capacity, part_width), "hid", axis=1, tiled=True),
    )
    gate_w = w_gate[0]
    up_w = w_up[0]
    down_w = w_down[0]
    gate_pre = contract_cols(rows_x, gate_w)
    up_pre = contract_cols(rows_x, up_w)
    expert_id = lax.axis_index("expert")
    unit_ids = lax.axis_index("hid") * local_units + jnp.arange(local_units, dtype=jnp.int32)
    row_ids = jnp.arange(capacity, dtype=jnp.int32)
    counter = (expert_id * capacity + row_ids[:, None]) * FF + unit_ids[None, :]
    keep_mul = keep_mask(counter, drop_seed[0], layer_id[0])
    logistic = jax.nn.sigmoid(gate_pre)
    swish = gate_pre * logistic
    hidden = (swish * up_pre * keep_mul).astype(jnp.bfloat16)
    grad_hidden = contract_cols(rows_dy, down_w) * keep_mul
    grad_upre = (grad_hidden * swish).astype(jnp.bfloat16)
    grad_gpre = (grad_hidden * up_pre * logistic * (1.0 + gate_pre * (1.0 - logistic))).astype(
        jnp.bfloat16
    )
    grad_down = contract_rows(hidden, rows_dy).astype(jnp.bfloat16)
    grad_gate = contract_rows(grad_gpre, rows_x).astype(jnp.bfloat16)
    grad_up = contract_rows(grad_upre, rows_x).astype(jnp.bfloat16)
    partial_sum = jnp.dot(grad_gpre, gate_w, preferred_element_type=jnp.float32) + jnp.dot(
        grad_upre, up_w, preferred_element_type=jnp.float32
    )
    summed = lax.psum(partial_sum.astype(jnp.bfloat16), "hid").astype(jnp.float32)
    own_cols = lax.dynamic_slice_in_dim(summed, lax.axis_index("hid") * part_width, part_width, 1)
    back_rows = lax.all_to_all(
        own_cols.astype(jnp.bfloat16).reshape(send_shape),
        "expert",
        split_axis=0,
        concat_axis=0,
        tiled=True,
    )
    grad_tokens = contract_rows(placed, back_rows.reshape(experts * CAP_SRC, part_width)).astype(
        jnp.bfloat16
    )
    return (grad_tokens, grad_gate[None], grad_up[None], grad_down[None])


def solution(mesh):
    in_specs = (
        P("expert", "hid"),
        P("expert", "hid"),
        P("expert", None),
        P("expert", None),
        P("expert", None),
        P(),
        P(),
        P("expert", "hid", None),
        P("expert", "hid", None),
        P("expert", "hid", None),
    )
    out_specs = (
        P("expert", "hid"),
        P("expert", "hid", None),
        P("expert", "hid", None),
        P("expert", "hid", None),
    )
    return jax.shard_map(
        on_device, mesh=mesh, in_specs=in_specs, out_specs=out_specs, check_vma=False
    )
```

profile of v0, /device:TPU:1, one launch (start us, length us, event | category | flops | bytes accessed | tf_op | source)
XLA Modules:
  0.0 131.4 jit_solution(13579242598336714023)
XLA Ops:
  7.2 0.0 copy-start
  7.2 0.7 add_select_fusion
  7.9 0.1 fusion.22
  8.0 0.8 select_reduce_fusion
  8.8 0.0 copy-done
  8.8 0.2 fusion.13
  9.1 0.5 broadcast.36
  9.6 1.3 reduce.4
  10.9 0.7 reshape.58
  11.6 6.4 %all-to-all-start = ((bf16[8,2,3584]{2,1,0:T(2,128)(2,1)}), bf16[8,2,3584]{2,1,0:T(2,128)(2,1)S(1)}, u32[]{:S(2)}, u32[]{:S(2)}) async-start(bf16[8,2,3584]{2,1,0:T(2,128)(2,1)} %reshape.58), calls=%async_computation | async-start | bytes 229376 | tf_op jit(solution)/shard_map/all_to_all | solution.py:58
  19.3 0.9 convolution_convert_fusion.3
  20.3 1.3 %reduce.3 = bf16[8,7168]{1,0:T(8,128)(2,1)S(1)} reduce(bf16[8,1,7168]{2,1,0:T(2,128)(2,1)S(1)} %all_to_all.25, bf16[]{:T(256)} %broadcast.36), dimensions={1}, to_apply=%all_to_all.25.reduce_sub_computation | reduce | bytes 229378 | tf_op jit(solution)/shard_map/all_to_all | solution.py:55
  21.6 0.7 reshape.56
  22.3 1.4 %all-to-all-done = bf16[8,2,3584]{2,1,0:T(2,128)(2,1)S(1)} async-done(((bf16[8,2,3584]{2,1,0:T(2,128)(2,1)}), bf16[8,2,3584]{2,1,0:T(2,128)(2,1)S(1)}, u32[]{:S(2)}, u32[]{:S(2)}) %all-to-all-start) | async-done | bytes 114720 | tf_op jit(solution)/shard_map/all_to_all | solution.py:58
  23.7 4.1 %all-to-all-start.1 = ((bf16[8,2,3584]{2,1,0:T(2,128)(2,1)}), bf16[8,2,3584]{2,1,0:T(2,128)(2,1)S(1)}, u32[]{:S(2)}, u32[]{:S(2)}) async-start(bf16[8,2,3584]{2,1,0:T(2,128)(2,1)} %reshape.56), calls=%async_computation.1 | async-start | bytes 229376 | tf_op jit(solution)/shard_map/all_to_all | solution.py:55
  27.8 0.0 all-reduce.2.cloned.1.call-start
  27.8 0.1 reshape.59
  27.9 0.7 reduce
  28.6 0.1 reshape.50
  28.7 4.9 %all-to-all-done.1 = bf16[8,2,3584]{2,1,0:T(2,128)(2,1)S(1)} async-done(((bf16[8,2,3584]{2,1,0:T(2,128)(2,1)}), bf16[8,2,3584]{2,1,0:T(2,128)(2,1)S(1)}, u32[]{:S(2)}, u32[]{:S(2)}) %all-to-all-start.1) | async-done | bytes 114720 | tf_op jit(solution)/shard_map/all_to_all | solution.py:55
  33.5 0.1 reshape.57
  33.6 0.7 reduce.1
  34.3 0.1 reshape.51
  34.4 0.0 copy-start.1
  34.4 0.0 copy-start.2
  34.4 8.3 %all_gather.7 = bf16[64,3584]{1,0:T(8,128)(2,1)S(1)} all-gather(bf16[64,896]{1,0:T(8,128)(2,1)S(1)} %reshape.51), channel_id=1, replica_groups=mesh['expert'=8,'hid'=4] {'hid'}, dimensions={1}, use_global_device_ids=true | all-gather | bytes 573440 | tf_op jit(solution)/shard_map/all_gather | solution.py:63
  42.7 0.0 slice-start
  42.7 4.0 %fusion.6 = f32[64,640]{1,0:T(8,128)S(1)} fusion(bf16[64,3584]{1,0:T(8,128)(2,1)S(1)} %all_gather.7, bf16[1,640,3584]{2,1,0:T(8,128)(2,1)} %param.17), kind=kOutput, calls=%fused_computation.10 | convolution fusion | flops 293601280 | bytes 5210112 | tf_op jit(solution)/shard_map/dot_general | solution.py:33
  46.7 0.0 copy-done.1
  46.7 0.0 slice-start.1
  46.7 1.5 %fusion.9 = f32[64,640]{1,0:T(8,128)S(1)} fusion(bf16[64,3584]{1,0:T(8,128)(2,1)S(1)} %all_gather.7, bf16[1,640,3584]{2,1,0:T(8,128)(2,1)S(1)} %copy-done.1), kind=kOutput, calls=%fused_computation.13 | convolution fusion | flops 293601280 | bytes 5210112 | tf_op jit(solution)/shard_map/dot_general | solution.py:33
  48.2 8.6 %all_gather.6 = bf16[64,3584]{1,0:T(8,128)(2,1)S(1)} all-gather(bf16[64,896]{1,0:T(8,128)(2,1)S(1)} %reshape.50), channel_id=1, replica_groups=mesh['expert'=8,'hid'=4] {'hid'}, dimensions={1}, use_global_device_ids=true | all-gather | bytes 573440 | tf_op jit(solution)/shard_map/all_gather | solution.py:64
  56.8 0.0 copy-done.2
  56.8 1.5 %multiply_convert_fusion = (bf16[64,640]{1,0:T(8,128)(2,1)S(1)}, bf16[64,640]{1,0:T(8,128)(2,1)S(1)}) fusion(f32[64,640]{1,0:T(8,128)S(1)} %fusion.6, f32[64,640]{1,0:T(8,128)S(1)} %fusion.9, s32[]{:T(128)} %bitcast.2, s32[]{:T(128)} %bitcast.1, s32[640]{0:T(1024)S(1)} %iota_add_fusion, s32[64]{0:T(128)S(1)} %add_multiply_fusion, ...), kind=kOutput, calls=%fused_computation.25 | convolution fusion | flops 294993920 | bytes 5540616 | tf_op jit(solution)/shard_map/dot_general | solution.py:33
  58.4 0.0 slice-done
  58.4 0.0 slice-done.1
  58.4 0.9 fusion.4
  59.3 1.7 %fusion.3 = bf16[64,3584]{1,0:T(8,128)(2,1)} fusion(f32[64,3584]{1,0:T(8,128)S(1)} %fusion.4, bf16[64,640]{1,0:T(8,128)(2,1)S(1)} %get-tuple-element.4, bf16[1,640,3584]{2,1,0:T(8,128)(2,1)S(1)} %copy-done.1), kind=kOutput, calls=%fused_computation.7 | convolution fusion | flops 294060032 | bytes 6045696 | tf_op jit(solution)/shard_map/dot_general | solution.py:87
  61.0 0.0 all-reduce.2.cloned.1.call-update
  61.0 3.5 %fusion.1 = bf16[1,640,3584]{2,1,0:T(8,128)(2,1)} fusion(bf16[64,640]{1,0:T(8,128)(2,1)S(1)} %get-tuple-element.4, bf16[64,3584]{1,0:T(8,128)(2,1)S(1)} %all_gather.7), kind=kOutput, calls=%fused_computation.4 | convolution fusion | flops 295895040 | bytes 5128192 | tf_op jit(solution)/shard_map/dot_general | solution.py:27
  64.6 42.6 %all-reduce.2.cloned.1.call-done = bf16[64,3584]{1,0:T(8,128)(2,1)} async-done(((bf16[64,3584]{1,0:T(8,128)(2,1)}), bf16[64,3584]{1,0:T(8,128)(2,1)}) %all-reduce.2.cloned.1.call-update) | async-done | bytes 458768 | tf_op jit(solution)/shard_map/psum | solution.py:90
  107.1 0.9 convert_convert_fusion
  108.1 1.3 %reduce.5 = bf16[8,7168]{1,0:T(8,128)(2,1)S(1)} reduce(bf16[8,1,7168]{2,1,0:T(2,128)(2,1)S(1)} %all_to_all.26, bf16[]{:T(256)} %broadcast.36), dimensions={1}, to_apply=%all_to_all.26.reduce_sub_computation | reduce | bytes 229378 | tf_op jit(solution)/shard_map/all_to_all | solution.py:92
  109.4 0.7 reshape.60
  110.1 5.7 %all-to-all-start.2 = ((bf16[8,2,3584]{2,1,0:T(2,128)(2,1)}), bf16[8,2,3584]{2,1,0:T(2,128)(2,1)S(1)}, u32[]{:S(2)}, u32[]{:S(2)}) async-start(bf16[8,2,3584]{2,1,0:T(2,128)(2,1)} %reshape.60), calls=%async_computation.2 | async-start | bytes 229376 | tf_op jit(solution)/shard_map/all_to_all | solution.py:92
  115.8 3.5 %fusion = bf16[1,640,3584]{2,1,0:T(8,128)(2,1)} fusion(bf16[64,640]{1,0:T(8,128)(2,1)S(1)} %get-tuple-element.5, bf16[64,3584]{1,0:T(8,128)(2,1)S(1)} %all_gather.7), kind=kOutput, calls=%fused_computation.3 | convolution fusion | flops 295895040 | bytes 5128192 | tf_op jit(solution)/shard_map/dot_general | solution.py:27
  119.3 3.6 %fusion.2 = bf16[1,640,3584]{2,1,0:T(8,128)(2,1)} fusion(bf16[64,3584]{1,0:T(8,128)(2,1)S(1)} %all_gather.6, f32[64,640]{1,0:T(8,128)S(1)} %fusion.9, s32[]{:T(128)} %bitcast.2, s32[]{:T(128)} %bitcast.1, s32[640]{0:T(1024)S(1)} %iota_add_fusion, s32[64]{0:T(128)S(1)} %add_multiply_fusion, f32[64,640]{1,0:T(8,128)S(1)} %fusion.6), kind=kOutput, calls=%fused_computation.5 | convolution fusion | flops 297000960 | bytes 5376776 | tf_op jit(solution)/shard_map/dot_general | solution.py:27
  123.0 0.0 all-to-all-done.2
  123.0 0.1 reshape.61
  123.1 0.6 reduce.2
  123.7 0.1 reshape.52
  123.8 0.7 convolution_convert_fusion.4
  (6 shorter events, 0.1 us)
Async XLA Ops:
  7.2 1.6 %copy-start = (bf16[8,896]{1,0:T(8,128)(2,1)S(1)}, bf16[8,896]{1,0:T(8,128)(2,1)}, u32[]{:S(2)}) copy-start(bf16[8,896]{1,0:T(8,128)(2,1)} %param.11) | copy-start | bytes 43012
  11.6 12.1 %all-to-all-start = ((bf16[8,2,3584]{2,1,0:T(2,128)(2,1)}), bf16[8,2,3584]{2,1,0:T(2,128)(2,1)S(1)}, u32[]{:S(2)}, u32[]{:S(2)}) async-start(bf16[8,2,3584]{2,1,0:T(2,128)(2,1)} %reshape.58), calls=%async_computation | async-start | bytes 229376 | tf_op jit(solution)/shard_map/all_to_all | solution.py:58
  23.7 9.9 %all-to-all-start.1 = ((bf16[8,2,3584]{2,1,0:T(2,128)(2,1)}), bf16[8,2,3584]{2,1,0:T(2,128)(2,1)S(1)}, u32[]{:S(2)}, u32[]{:S(2)}) async-start(bf16[8,2,3584]{2,1,0:T(2,128)(2,1)} %reshape.56), calls=%async_computation.1 | async-start | bytes 229376 | tf_op jit(solution)/shard_map/all_to_all | solution.py:55
  27.8 79.3 %all-reduce.2.cloned.1.call-start = ((), (), s32[]{:S(2)}) async-start(), calls=%async_computation.3 | async-start | bytes 917504 | tf_op jit(solution)/shard_map/psum | solution.py:90
  34.4 12.3 %copy-start.1 = (bf16[1,640,3584]{2,1,0:T(8,128)(2,1)S(1)}, bf16[1,640,3584]{2,1,0:T(8,128)(2,1)}, u32[]{:S(2)}) copy-start(bf16[1,640,3584]{2,1,0:T(8,128)(2,1)} %param.18) | copy-start | bytes 13762564
  34.4 22.5 %copy-start.2 = (bf16[1,640,3584]{2,1,0:T(8,128)(2,1)S(1)}, bf16[1,640,3584]{2,1,0:T(8,128)(2,1)}, u32[]{:S(2)}) copy-start(bf16[1,640,3584]{2,1,0:T(8,128)(2,1)} %param.19) | copy-start | bytes 13762564
  42.7 15.7 %slice-start = ((s8[4587520]{0:T(1024)(128)(4,1)}), s8[4194304]{0:T(1024)(128)(4,1)S(1)}, s32[]{:S(2)}) async-start(s8[4587520]{0:T(1024)(128)(4,1)} %bitcast.41), calls=%async_computation.4 | async-start | bytes 8388608
  46.7 11.7 %slice-start.1 = ((s8[4587520]{0:T(1024)(128)(4,1)}), s8[393216]{0:T(1024)(128)(4,1)S(1)}, s32[]{:S(2)}) async-start(s8[4587520]{0:T(1024)(128)(4,1)} %bitcast.41), calls=%async_computation.5 | async-start | bytes 786432
  110.1 12.9 %all-to-all-start.2 = ((bf16[8,2,3584]{2,1,0:T(2,128)(2,1)}), bf16[8,2,3584]{2,1,0:T(2,128)(2,1)S(1)}, u32[]{:S(2)}, u32[]{:S(2)}) async-start(bf16[8,2,3584]{2,1,0:T(2,128)(2,1)} %reshape.60), calls=%async_computation.2 | async-start | bytes 229376 | tf_op jit(solution)/shard_map/all_to_all | solution.py:92
Sparse Core Ops, SparseCore 0:
  61.2 45.9 all-reduce.1
where the time goes:
time: 132 us; the launch traced here: 131 us
  waiting for transfers between devices  48.8 us (37%)
  matrix products  22.2 us (17%)
  blocking collectives  16.9 us (13%)
  starting transfers between devices  16.2 us (12%)
  between operations  15.5 us (12%)
  other arithmetic  8.46 us (6%)
  local copies, waits for them, and re-layouts  3.23 us (2%)
    psum x1, waiting for transfers between devices, on_device(): lax.psum(partial_sum.astype(jnp.bfloat16), 'hid').astype(jnp.float32)  42.6 us
    dot_general x4, matrix products, contract_rows(): lax.dot_general(left, right, (((0,), (0,)), ((), ())), preferred_element_...  11.4 us
    all_gather x1, blocking collectives, on_device(): lax.all_gather(recv_dy.reshape(capacity, part_width), 'hid', axis=1, tile...  8.65 us
    all_gather x1, blocking collectives, on_device(): lax.all_gather(recv_x.reshape(capacity, part_width), 'hid', axis=1, tiled...  8.3 us
    dot_general x3, matrix products, contract_cols(): lax.dot_general(left, right, (((1,), (1,)), ((), ())), preferred_element_...  6.98 us
    all_to_all x1, starting transfers between devices, on_device(): lax.all_to_all(sent_dy.reshape(send_shape), 'expert', split_axis=0, conca...  6.38 us
    all_to_all x1, starting transfers between devices, on_device(): lax.all_to_all(own_cols.astype(jnp.bfloat16).reshape(send_shape), 'expert...  5.71 us
    all_to_all x1, waiting for transfers between devices, on_device(): lax.all_to_all(sent_x.reshape(send_shape), 'expert', split_axis=0, concat...  4.86 us
  transfers between devices with their start and end apart: 4, of which 3 were waited for; matrix products, arithmetic and copies ran while one was open for 11% of the time, Pallas kernels for 0%

commit v1 on v0

--- a/solution.py
+++ b/solution.py
@@ -6,6 +6,18 @@
 FF = 2560
 CAP_SRC = 8
 KEEP_FACTOR = 1024.0 / 922.0
+
+
+def doubled_up(array, axis, dim):
+    ways, here = (lax.axis_size(axis), lax.axis_index(axis))
+    grown, reach = (array, 1)
+    while reach < ways:
+        theirs = lax.ppermute(grown, axis, [(d, d ^ reach) for d in range(ways)])
+        mine_first = jnp.concatenate([grown, theirs], axis=dim)
+        theirs_first = jnp.concatenate([theirs, grown], axis=dim)
+        grown = jnp.where(here & reach == 0, mine_first, theirs_first)
+        reach = 2 * reach
+    return grown
 
 
 def logical_shift(values, amount):
@@ -60,7 +72,7 @@
         ),
     )
     rows_x, rows_dy = (
-        lax.all_gather(recv_x.reshape(capacity, part_width), "hid", axis=1, tiled=True),
+        doubled_up(recv_x.reshape(capacity, part_width), "hid", 1),
         lax.all_gather(recv_dy.reshape(capacity, part_width), "hid", axis=1, tiled=True),
     )
     gate_w = w_gate[0]

time: 132 us -> 127 us (0.962)
  blocking collectives: 16.9 us -> 8.3 us
  starting transfers between devices: 16.2 us -> 19.1 us
    all_gather x1 -> x0, blocking collectives: 8.3 us -> none  [on_device(): lax.all_gather(recv_x.reshape(capacity, part_width), 'hid', axis=1, tiled...]
    ppermute x0 -> x2, starting transfers between devices: none -> 2.58 us  [doubled_up(): theirs = lax.ppermute(grown, axis, [(d, d ^ reach) for d in range(ways)])]
    all_to_all x1, starting transfers between devices: 4.14 us -> 6.38 us  [on_device(): lax.all_to_all(sent_x.reshape(send_shape), 'expert', split_axis=0, concat...]
    all_to_all x1, starting transfers between devices: 6.38 us -> 4.42 us  [on_device(): lax.all_to_all(sent_dy.reshape(send_shape), 'expert', split_axis=0, conca...]
    all_to_all x1, waiting for transfers between devices: 1.36 us -> 3.03 us  [on_device(): lax.all_to_all(sent_dy.reshape(send_shape), 'expert', split_axis=0, conca...]
    psum x1, waiting for transfers between devices: 42.6 us -> 41.2 us  [on_device(): lax.psum(partial_sum.astype(jnp.bfloat16), 'hid').astype(jnp.float32)]
  transfers between devices with their start and end apart: 4 -> 6, of which waited for: 3 -> 3; matrix products, arithmetic and copies ran while one was open for 11% -> 12% of each run, Pallas kernels for 0% -> 0%
where the time goes in v1:
time: 127 us; the launch traced here: 126 us
  waiting for transfers between devices  49.1 us (39%)
  matrix products  22.2 us (17%)
  starting transfers between devices  19.1 us (15%)
  between operations  15.5 us (12%)
  other arithmetic  8.52 us (7%)
  blocking collectives  8.3 us (7%)
  local copies, waits for them, and re-layouts  3.23 us (3%)
    psum x1, waiting for transfers between devices, on_device(): lax.psum(partial_sum.astype(jnp.bfloat16), 'hid').astype(jnp.float32)  41.2 us
    dot_general x4, matrix products, contract_rows(): lax.dot_general(left, right, (((0,), (0,)), ((), ())), preferred_element_...  11.4 us
    all_gather x1, blocking collectives, on_device(): lax.all_gather(recv_dy.reshape(capacity, part_width), 'hid', axis=1, tile...  8.3 us
    dot_general x3, matrix products, contract_cols(): lax.dot_general(left, right, (((1,), (1,)), ((), ())), preferred_element_...  6.97 us
    all_to_all x1, starting transfers between devices, on_device(): lax.all_to_all(sent_x.reshape(send_shape), 'expert', split_axis=0, concat...  6.38 us
    all_to_all x1, starting transfers between devices, on_device(): lax.all_to_all(own_cols.astype(jnp.bfloat16).reshape(send_shape), 'expert...  5.71 us
    all_to_all x1, waiting for transfers between devices, on_device(): lax.all_to_all(sent_x.reshape(send_shape), 'expert', split_axis=0, concat...  4.91 us
    all_to_all x1, starting transfers between devices, on_device(): lax.all_to_all(sent_dy.reshape(send_shape), 'expert', split_axis=0, conca...  4.42 us
  transfers between devices with their start and end apart: 6, of which 3 were waited for; matrix products, arithmetic and copies ran while one was open for 12% of the time, Pallas kernels for 0%

profile of v1, /device:TPU:1, one launch (start us, length us, event | category | flops | bytes accessed | tf_op | source)
XLA Modules:
  0.0 126.0 jit_solution(16257892778137474524)
XLA Ops:
  7.2 0.0 copy-start
  7.2 0.7 add_select_fusion
  7.9 0.1 fusion.22
  8.0 0.0 copy-done
  8.0 0.2 convolution_convert_fusion.3
  8.3 0.5 broadcast.36
  8.8 1.3 %reduce.3 = bf16[8,7168]{1,0:T(8,128)(2,1)S(1)} reduce(bf16[8,1,7168]{2,1,0:T(2,128)(2,1)S(1)} %all_to_all.25, bf16[]{:T(256)} %broadcast.36), dimensions={1}, to_apply=%all_to_all.25.reduce_sub_computation | reduce | bytes 229378 | tf_op jit(solution)/shard_map/all_to_all | solution.py:67
  10.1 0.7 reshape.56
  10.8 6.4 %all-to-all-start.1 = ((bf16[8,2,3584]{2,1,0:T(2,128)(2,1)}), bf16[8,2,3584]{2,1,0:T(2,128)(2,1)S(1)}, u32[]{:S(2)}, u32[]{:S(2)}) async-start(bf16[8,2,3584]{2,1,0:T(2,128)(2,1)} %reshape.56), calls=%async_computation.1 | async-start | bytes 229376 | tf_op jit(solution)/shard_map/all_to_all | solution.py:67
  17.2 0.8 select_reduce_fusion
  18.0 4.9 %all-to-all-done.1 = bf16[8,2,3584]{2,1,0:T(2,128)(2,1)S(1)} async-done(((bf16[8,2,3584]{2,1,0:T(2,128)(2,1)}), bf16[8,2,3584]{2,1,0:T(2,128)(2,1)S(1)}, u32[]{:S(2)}, u32[]{:S(2)}) %all-to-all-start.1) | async-done | bytes 114720 | tf_op jit(solution)/shard_map/all_to_all | solution.py:67
  22.9 0.1 reshape.57
  23.0 0.7 reduce.1
  23.7 0.1 reshape.51
  23.7 1.3 %collective-permute-start = (bf16[64,896]{1,0:T(8,128)(2,1)S(1)}, bf16[64,896]{1,0:T(8,128)(2,1)S(1)}, u32[]{:S(2)}, u32[]{:S(2)}) collective-permute-start(bf16[64,896]{1,0:T(8,128)(2,1)S(1)} %reshape.51), channel_id=1, source_target_pairs={{0,1},{1,0},{2,3},{3,2},{4,5},{5,4},{6,7},{7,6},{8,9},{9,8},{10,11... | collective-permute-start | bytes 344072 | tf_op jit(solution)/shard_map/ppermute | solution.py:15
  25.0 0.9 fusion.13
  26.0 1.3 %reduce.4 = bf16[8,7168]{1,0:T(8,128)(2,1)S(1)} reduce(bf16[8,1,7168]{2,1,0:T(2,128)(2,1)S(1)} %all_to_all.24, bf16[]{:T(256)} %broadcast.36), dimensions={1}, to_apply=%all_to_all.24.reduce_sub_computation | reduce | bytes 229378 | tf_op jit(solution)/shard_map/all_to_all | solution.py:70
  27.3 0.7 reshape.58
  28.0 4.4 %all-to-all-start = ((bf16[8,2,3584]{2,1,0:T(2,128)(2,1)}), bf16[8,2,3584]{2,1,0:T(2,128)(2,1)S(1)}, u32[]{:S(2)}, u32[]{:S(2)}) async-start(bf16[8,2,3584]{2,1,0:T(2,128)(2,1)} %reshape.58), calls=%async_computation | async-start | bytes 229376 | tf_op jit(solution)/shard_map/all_to_all | solution.py:70
  32.4 0.0 all-reduce.2.cloned.1.call-start
  32.5 0.0 collective-permute-done
  32.5 0.1 maximum_select_fusion.1
  32.5 1.3 %collective-permute-start.1 = (bf16[64,1792]{1,0:T(8,128)(2,1)S(1)}, bf16[64,1792]{1,0:T(8,128)(2,1)S(1)}, u32[]{:S(2)}, u32[]{:S(2)}) collective-permute-start(bf16[64,1792]{1,0:T(8,128)(2,1)S(1)} %maximum_select_fusion.1), channel_id=1, source_target_pairs={{0,2},{1,3},{2,0},{3,1},{4,6},{5,7},{6,4},{7,5},{8,10},{9,11},{10,... | collective-permute-start | bytes 688136 | tf_op jit(solution)/shard_map/ppermute | solution.py:15
  35.1 3.0 %all-to-all-done = bf16[8,2,3584]{2,1,0:T(2,128)(2,1)S(1)} async-done(((bf16[8,2,3584]{2,1,0:T(2,128)(2,1)}), bf16[8,2,3584]{2,1,0:T(2,128)(2,1)S(1)}, u32[]{:S(2)}, u32[]{:S(2)}) %all-to-all-start) | async-done | bytes 114720 | tf_op jit(solution)/shard_map/all_to_all | solution.py:70
  38.2 0.1 reshape.59
  38.3 0.7 reduce
  39.0 0.1 reshape.50
  39.0 0.0 copy-start.1
  39.0 8.3 %all_gather.3 = bf16[64,3584]{1,0:T(8,128)(2,1)S(1)} all-gather(bf16[64,896]{1,0:T(8,128)(2,1)S(1)} %reshape.50), channel_id=1, replica_groups=mesh['expert'=8,'hid'=4] {'hid'}, dimensions={1}, use_global_device_ids=true | all-gather | bytes 573440 | tf_op jit(solution)/shard_map/all_gather | solution.py:76
  47.3 0.0 copy-start.2
  47.3 0.0 collective-permute-done.1
  47.3 0.0 slice-start
  47.3 3.9 %fusion.6 = f32[64,640]{1,0:T(8,128)S(1)} fusion(bf16[1,640,3584]{2,1,0:T(8,128)(2,1)} %param.17, bf16[64,1792]{1,0:T(8,128)(2,1)S(1)} %collective-permute-done.1, bf16[64,1792]{1,0:T(8,128)(2,1)S(1)} %maximum_select_fusion.1, pred[]{:T(512)S(6)} %eq.22), kind=kOutput, calls=%fused_computation.10 | convolution fusion | flops 295665664 | bytes 5210113 | tf_op jit(solution)/shard_map/dot_general | solution.py:45
  51.3 0.0 copy-done.1
  51.3 0.0 slice-start.1
  51.3 1.5 %fusion.9 = f32[64,640]{1,0:T(8,128)S(1)} fusion(bf16[1,640,3584]{2,1,0:T(8,128)(2,1)S(1)} %copy-done.1, bf16[64,1792]{1,0:T(8,128)(2,1)S(1)} %collective-permute-done.1, bf16[64,1792]{1,0:T(8,128)(2,1)S(1)} %maximum_select_fusion.1, pred[]{:T(512)S(6)} %eq.22), kind=kOutput, calls=%fused_computation.13 | convolution fusion | flops 295665664 | bytes 5210113 | tf_op jit(solution)/shard_map/dot_general | solution.py:45
  52.8 0.0 copy-done.2
  52.9 1.5 %multiply_convert_fusion = (bf16[64,640]{1,0:T(8,128)(2,1)S(1)}, bf16[64,640]{1,0:T(8,128)(2,1)S(1)}) fusion(f32[64,640]{1,0:T(8,128)S(1)} %fusion.6, f32[64,640]{1,0:T(8,128)S(1)} %fusion.9, s32[]{:T(128)} %bitcast.2, s32[]{:T(128)} %bitcast.1, s32[640]{0:T(1024)S(1)} %iota_add_fusion, s32[64]{0:T(128)S(1)} %add_multiply_fusion, ...), kind=kOutput, calls=%fused_computation.27 | convolution fusion | flops 294993920 | bytes 5540616 | tf_op jit(solution)/shard_map/dot_general | solution.py:45
  54.4 0.0 slice-done
  54.4 0.0 slice-done.1
  54.4 0.9 fusion.4
  55.3 1.7 %fusion.3 = bf16[64,3584]{1,0:T(8,128)(2,1)} fusion(f32[64,3584]{1,0:T(8,128)S(1)} %fusion.4, bf16[64,640]{1,0:T(8,128)(2,1)S(1)} %get-tuple-element.4, bf16[1,640,3584]{2,1,0:T(8,128)(2,1)S(1)} %copy-done.1), kind=kOutput, calls=%fused_computation.7 | convolution fusion | flops 294060032 | bytes 6045696 | tf_op jit(solution)/shard_map/dot_general | solution.py:99
  57.0 0.0 all-reduce.2.cloned.1.call-update
  57.1 3.5 %fusion.1 = bf16[1,640,3584]{2,1,0:T(8,128)(2,1)} fusion(bf16[64,640]{1,0:T(8,128)(2,1)S(1)} %get-tuple-element.4, bf16[64,1792]{1,0:T(8,128)(2,1)S(1)} %collective-permute-done.1, bf16[64,1792]{1,0:T(8,128)(2,1)S(1)} %maximum_select_fusion.1, pred[]{:T(512)S(6)} %eq.22), kind=kOutput, calls=%fused_computation.4 | convolution fusion | flops 297959424 | bytes 5128193 | tf_op jit(solution)/shard_map/dot_general | solution.py:39
  60.6 41.2 %all-reduce.2.cloned.1.call-done = bf16[64,3584]{1,0:T(8,128)(2,1)} async-done(((bf16[64,3584]{1,0:T(8,128)(2,1)}), bf16[64,3584]{1,0:T(8,128)(2,1)}) %all-reduce.2.cloned.1.call-update) | async-done | bytes 458768 | tf_op jit(solution)/shard_map/psum | solution.py:102
  101.8 0.9 convert_convert_fusion
  102.7 1.3 %reduce.5 = bf16[8,7168]{1,0:T(8,128)(2,1)S(1)} reduce(bf16[8,1,7168]{2,1,0:T(2,128)(2,1)S(1)} %all_to_all.26, bf16[]{:T(256)} %broadcast.36), dimensions={1}, to_apply=%all_to_all.26.reduce_sub_computation | reduce | bytes 229378 | tf_op jit(solution)/shard_map/all_to_all | solution.py:104
  104.0 0.7 reshape.60
  104.7 5.7 %all-to-all-start.2 = ((bf16[8,2,3584]{2,1,0:T(2,128)(2,1)}), bf16[8,2,3584]{2,1,0:T(2,128)(2,1)S(1)}, u32[]{:S(2)}, u32[]{:S(2)}) async-start(bf16[8,2,3584]{2,1,0:T(2,128)(2,1)} %reshape.60), calls=%async_computation.2 | async-start | bytes 229376 | tf_op jit(solution)/shard_map/all_to_all | solution.py:104
  110.5 3.5 %fusion = bf16[1,640,3584]{2,1,0:T(8,128)(2,1)} fusion(bf16[64,640]{1,0:T(8,128)(2,1)S(1)} %get-tuple-element.5, bf16[64,1792]{1,0:T(8,128)(2,1)S(1)} %collective-permute-done.1, bf16[64,1792]{1,0:T(8,128)(2,1)S(1)} %maximum_select_fusion.1, pred[]{:T(512)S(6)} %eq.22), kind=kOutput, calls=%fused_computation.3 | convolution fusion | flops 297959424 | bytes 5128193 | tf_op jit(solution)/shard_map/dot_general | solution.py:39
  114.0 3.6 %fusion.2 = bf16[1,640,3584]{2,1,0:T(8,128)(2,1)} fusion(bf16[64,3584]{1,0:T(8,128)(2,1)S(1)} %all_gather.3, f32[64,640]{1,0:T(8,128)S(1)} %fusion.9, s32[]{:T(128)} %bitcast.2, s32[]{:T(128)} %bitcast.1, s32[640]{0:T(1024)S(1)} %iota_add_fusion, s32[64]{0:T(128)S(1)} %add_multiply_fusion, f32[64,640]{1,0:T(8,128)S(1)} %fusion.6), kind=kOutput, calls=%fused_computation.5 | convolution fusion | flops 297000960 | bytes 5376776 | tf_op jit(solution)/shard_map/dot_general | solution.py:39
  117.6 0.0 all-to-all-done.2
  117.6 0.1 reshape.61
  117.7 0.6 reduce.2
  118.4 0.1 reshape.52
  118.4 0.7 convolution_convert_fusion.4
  (6 shorter events, 0.1 us)
Async XLA Ops:
  7.2 0.8 copy-start
  10.8 12.1 %all-to-all-start.1 = ((bf16[8,2,3584]{2,1,0:T(2,128)(2,1)}), bf16[8,2,3584]{2,1,0:T(2,128)(2,1)S(1)}, u32[]{:S(2)}, u32[]{:S(2)}) async-start(bf16[8,2,3584]{2,1,0:T(2,128)(2,1)} %reshape.56), calls=%async_computation.1 | async-start | bytes 229376 | tf_op jit(solution)/shard_map/all_to_all | solution.py:67
  23.7 8.7 %collective-permute-start = (bf16[64,896]{1,0:T(8,128)(2,1)S(1)}, bf16[64,896]{1,0:T(8,128)(2,1)S(1)}, u32[]{:S(2)}, u32[]{:S(2)}) collective-permute-start(bf16[64,896]{1,0:T(8,128)(2,1)S(1)} %reshape.51), channel_id=1, source_target_pairs={{0,1},{1,0},{2,3},{3,2},{4,5},{5,4},{6,7},{7,6},{8,9},{9,8},{10,11... | collective-permute-start | bytes 344072 | tf_op jit(solution)/shard_map/ppermute | solution.py:15
  28.0 10.1 %all-to-all-start = ((bf16[8,2,3584]{2,1,0:T(2,128)(2,1)}), bf16[8,2,3584]{2,1,0:T(2,128)(2,1)S(1)}, u32[]{:S(2)}, u32[]{:S(2)}) async-start(bf16[8,2,3584]{2,1,0:T(2,128)(2,1)} %reshape.58), calls=%async_computation | async-start | bytes 229376 | tf_op jit(solution)/shard_map/all_to_all | solution.py:70
  32.4 69.3 %all-reduce.2.cloned.1.call-start = ((), (), s32[]{:S(2)}) async-start(), calls=%async_computation.3 | async-start | bytes 917504 | tf_op jit(solution)/shard_map/psum | solution.py:102
  32.5 14.8 %collective-permute-start.1 = (bf16[64,1792]{1,0:T(8,128)(2,1)S(1)}, bf16[64,1792]{1,0:T(8,128)(2,1)S(1)}, u32[]{:S(2)}, u32[]{:S(2)}) collective-permute-start(bf16[64,1792]{1,0:T(8,128)(2,1)S(1)} %maximum_select_fusion.1), channel_id=1, source_target_pairs={{0,2},{1,3},{2,0},{3,1},{4,6},{5,7},{6,4},{7,5},{8,10},{9,11},{10,... | collective-permute-start | bytes 688136 | tf_op jit(solution)/shard_map/ppermute | solution.py:15
  39.0 12.3 %copy-start.1 = (bf16[1,640,3584]{2,1,0:T(8,128)(2,1)S(1)}, bf16[1,640,3584]{2,1,0:T(8,128)(2,1)}, u32[]{:S(2)}) copy-start(bf16[1,640,3584]{2,1,0:T(8,128)(2,1)} %param.18) | copy-start | bytes 13762564
  47.3 5.5 %copy-start.2 = (bf16[1,640,3584]{2,1,0:T(8,128)(2,1)S(1)}, bf16[1,640,3584]{2,1,0:T(8,128)(2,1)}, u32[]{:S(2)}) copy-start(bf16[1,640,3584]{2,1,0:T(8,128)(2,1)} %param.19) | copy-start | bytes 13762564
  47.3 7.0 %slice-start = ((s8[4587520]{0:T(1024)(128)(4,1)}), s8[4194304]{0:T(1024)(128)(4,1)S(1)}, s32[]{:S(2)}) async-start(s8[4587520]{0:T(1024)(128)(4,1)} %bitcast.37), calls=%async_computation.4 | async-start | bytes 8388608
  51.3 3.1 %slice-start.1 = ((s8[4587520]{0:T(1024)(128)(4,1)}), s8[393216]{0:T(1024)(128)(4,1)S(1)}, s32[]{:S(2)}) async-start(s8[4587520]{0:T(1024)(128)(4,1)} %bitcast.37), calls=%async_computation.5 | async-start | bytes 786432
  104.7 12.9 %all-to-all-start.2 = ((bf16[8,2,3584]{2,1,0:T(2,128)(2,1)}), bf16[8,2,3584]{2,1,0:T(2,128)(2,1)S(1)}, u32[]{:S(2)}, u32[]{:S(2)}) async-start(bf16[8,2,3584]{2,1,0:T(2,128)(2,1)} %reshape.60), calls=%async_computation.2 | async-start | bytes 229376 | tf_op jit(solution)/shard_map/all_to_all | solution.py:104
Sparse Core Ops, SparseCore 0:
  57.2 44.5 all-reduce.1
